TPU v7x, 512 devices: a whole 4x4x16 slice. The times are simulated.
512 devices in a mesh: dom: 64 (over z, y), rep: 8 (over x, core).
Axes of the slice: x: 4, y: 4, z: 16, core: 2. Of those that a mesh axis runs over, the one named last changes fastest.
Arguments:
- feats: bfloat16 [65536, 128], P(('dom', 'rep')), may hold values from -6 to 6
- weight: bfloat16 [128, 128], replicated, may hold values from -0.5 to 0.5
- bias: float32 [128], replicated, may hold values from -3 to 3
- tiles: bfloat16 [512, 5, 28, 128, 128], P(('dom', 'rep')), may hold values from -0.0625 to 0.0625
- tile_cols: int32 [512, 5, 28], P(('dom', 'rep')), may hold values from 0 to 7
- tile_count: int32 [512, 5], P(('dom', 'rep')), may hold values from 2 to 28, as said below
- cotangent: bfloat16 [65536, 128], P(('dom', 'rep')), may hold values from -6 to 6
Outputs:
- hidden: bfloat16 [65536, 128], P(('dom', 'rep'))
- grad_weight: float32 [128, 128], replicated
- grad_bias: float32 [128], replicated
- grad_feats: bfloat16 [65536, 128], P(('dom', 'rep'))
Inputs may be any that keep to these rules, and one draw needn't show every extreme that they name: `tile_count`: every list has at least two live tiles; the nodes of some device have 28 live tiles in every list, and those of most devices far fewer.
All inputs are finite; a program needn't handle non-finite values.
Results may differ from a plain program's by a relative error of at most 0.0062.
Values may be sent and summed in bfloat16 or wider, within the bound.
A program may use at most 64 MiB of HBM per device.

v0:
```python
import jax
import jax.numpy as jnp
from jax import lax
from jax.sharding import PartitionSpec as P


def swapped(value, axis, bit):
    mask = 2**bit
    pairs = [(source, source ^ mask) for source in range(lax.axis_size(axis))]
    return lax.ppermute(value, axis, pairs)


def gelu_tanh(values):
    return jax.nn.gelu(values, approximate=True)


def add_slot(summed, panel, slot, tiles, tile_cols, live_mask):
    tgt_blocks, slot_count, max_tiles, block, unused = tiles.shape
    width = panel.shape[1]
    panel_blocks = panel.shape[0] // block
    source = panel.reshape(panel_blocks, block, width)
    columns = tile_cols[:, slot]
    slot_tiles = tiles[:, slot]
    fetched = source[columns]
    fetched = jnp.where(live_mask[:, slot][:, :, None, None], fetched, jnp.zeros((), jnp.bfloat16))
    return summed + jnp.einsum(
        "tmij,tmjh->tih", slot_tiles, fetched, preferred_element_type=jnp.float32
    )


def partial_panel(slot, tiles, tile_cols, live_mask, grad_rows_b, panel_blocks):
    tgt_blocks, slot_count, max_tiles, block, unused = tiles.shape
    width = grad_rows_b.shape[2]
    masked = jnp.where(
        live_mask[:, slot][:, :, None, None], tiles[:, slot], jnp.zeros((), jnp.bfloat16)
    )
    contrib = jnp.einsum("tmij,tih->tmjh", masked, grad_rows_b, preferred_element_type=jnp.float32)
    targets = tile_cols[:, slot].reshape(tgt_blocks * max_tiles)
    placed = jnp.zeros((panel_blocks, block, width), jnp.float32)
    placed = placed.at[targets].add(contrib.reshape(tgt_blocks * max_tiles, block, width))
    return placed.reshape(panel_blocks * block, width)


def body(feats, weight, bias, tiles, tile_cols, tile_count, cotangent):
    dom_size = lax.axis_size("dom")
    rep_size = lax.axis_size("rep")
    top_bit = dom_size.bit_length() - 1
    tgt_blocks, slot_count, max_tiles, block, unused = tiles.shape
    width = weight.shape[1]
    panel_blocks = rep_size * tgt_blocks
    live_mask = jnp.arange(max_tiles)[None, None, :] < tile_count[:, :, None]
    projected = jnp.dot(feats, weight, preferred_element_type=jnp.float32).astype(jnp.bfloat16)
    own_rows = lax.all_gather(projected, "rep", axis=0, tiled=True)
    summed = jnp.zeros((tgt_blocks, block, width), jnp.float32)
    summed = add_slot(summed, own_rows, 0, tiles, tile_cols, live_mask)
    for round_index in range(1, slot_count):
        bit_number = top_bit - round_index
        partner_rows = swapped(own_rows, "dom", bit_number)
        summed = add_slot(summed, partner_rows, round_index, tiles, tile_cols, live_mask)
    preact = summed.reshape(tgt_blocks * block, width) + bias
    hidden_f, pullback = jax.vjp(gelu_tanh, preact)
    hidden = hidden_f.astype(jnp.bfloat16)
    grad_pre = pullback(cotangent.astype(jnp.float32))[0]
    grad_rows_b = grad_pre.astype(jnp.bfloat16).reshape(tgt_blocks, block, width)
    grad_panel = partial_panel(0, tiles, tile_cols, live_mask, grad_rows_b, panel_blocks)
    for round_index in range(1, slot_count):
        outgoing = partial_panel(
            round_index, tiles, tile_cols, live_mask, grad_rows_b, panel_blocks
        )
        grad_panel = grad_panel + swapped(outgoing, "dom", top_bit - round_index)
    grad_proj = lax.psum_scatter(grad_panel, "rep", scatter_dimension=0, tiled=True).astype(
        jnp.bfloat16
    )
    weight_local = lax.dot_general(
        feats, grad_proj, (((0,), (0,)), ((), ())), preferred_element_type=jnp.float32
    )
    bias_local = jnp.sum(grad_pre, axis=0)
    grad_weight, grad_bias = lax.psum((weight_local, bias_local), ("dom", "rep"))
    grad_feats = lax.dot_general(
        grad_proj, weight, (((1,), (1,)), ((), ())), preferred_element_type=jnp.float32
    ).astype(jnp.bfloat16)
    return (hidden, grad_weight, grad_bias, grad_feats)


def solution(mesh):
    return jax.shard_map(
        body,
        mesh=mesh,
        in_specs=(
            P(("dom", "rep"), None),
            P(),
            P(),
            P(("dom", "rep"), None, None, None, None),
            P(("dom", "rep"), None, None),
            P(("dom", "rep"), None),
            P(("dom", "rep"), None),
        ),
        out_specs=(P(("dom", "rep"), None), P(), P(), P(("dom", "rep"), None)),
        check_vma=False,
    )
```

profile of v0, /device:TPU:1, one launch (start us, length us, event | category | flops | bytes accessed | tf_op | source)
XLA Modules:
  0.0 770.6 jit_solution(12770402989602264046)
XLA Ops:
  8.8 19.5 %all_gather.3 = bf16[1024,128]{1,0:T(8,128)(2,1)S(1)} all-gather(bf16[128,128]{1,0:T(8,128)(2,1)S(1)} %convolution_convert_fusion.1), channel_id=1, replica_groups=mesh['dom'=64,'rep'=8] {'rep'}, dimensions={0}, use_global_device_ids=true | all-gather | bytes 294912 | tf_op jit(solution)/shard_map/all_gather | solution.py:53
  28.3 1.9 collective-permute-start.3
  30.2 1.9 collective-permute-start.2
  32.2 8.4 %collective-permute-start.1 = (bf16[1024,128]{1,0:T(8,128)(2,1)S(1)}, bf16[1024,128]{1,0:T(8,128)(2,1)S(1)}, u32[]{:S(2)}, u32[]{:S(2)}) collective-permute-start(bf16[1024,128]{1,0:T(8,128)(2,1)S(1)} %all_gather.3), channel_id=1, source_target_pairs={{0,128},{8,136},{16,144},{24,152},{32,160},{40,168},{48,176},{56,1... | collective-permute-start | bytes 786440 | tf_op jit(solution)/shard_map/ppermute | solution.py:10
  40.6 7.9 %collective-permute-start = (bf16[1024,128]{1,0:T(8,128)(2,1)S(1)}, bf16[1024,128]{1,0:T(8,128)(2,1)S(1)}, u32[]{:S(2)}, u32[]{:S(2)}) collective-permute-start(bf16[1024,128]{1,0:T(8,128)(2,1)S(1)} %all_gather.3), channel_id=1, source_target_pairs={{0,256},{8,264},{16,272},{24,280},{32,288},{40,296},{48,304},{56,3... | collective-permute-start | bytes 786440 | tf_op jit(solution)/shard_map/ppermute | solution.py:10
  51.5 1.6 convolution_bitcast_fusion.4
  53.9 1.6 convolution_bitcast_fusion
  55.6 8.0 %collective-permute-done.2 = bf16[1024,128]{1,0:T(8,128)(2,1)S(1)} collective-permute-done((bf16[1024,128]{1,0:T(8,128)(2,1)S(1)}, bf16[1024,128]{1,0:T(8,128)(2,1)S(1)}, u32[]{:S(2)}, u32[]{:S(2)}) %collective-permute-start.2) | collective-permute-done | bytes 262176 | tf_op jit(solution)/shard_map/ppermute | solution.py:10
  64.3 1.6 convolution_bitcast_fusion.1
  66.0 19.9 %collective-permute-done.1 = bf16[1024,128]{1,0:T(8,128)(2,1)S(1)} collective-permute-done((bf16[1024,128]{1,0:T(8,128)(2,1)S(1)}, bf16[1024,128]{1,0:T(8,128)(2,1)S(1)}, u32[]{:S(2)}, u32[]{:S(2)}) %collective-permute-start.1) | collective-permute-done | bytes 262176 | tf_op jit(solution)/shard_map/ppermute | solution.py:10
  86.7 1.6 convolution_bitcast_fusion.2
  89.1 2.3 fusion.100
  91.4 3.2 fusion.12
  94.6 3.2 fusion.10
  97.8 2.0 fusion.8
  99.8 3.2 fusion.6
  103.0 4.6 scatter_fusion.1
  107.6 11.3 %collective-permute-start.4 = (f32[1024,128]{1,0:T(8,128)S(1)}, f32[1024,128]{1,0:T(8,128)}, u32[]{:S(2)}, u32[]{:S(2)}) collective-permute-start(f32[1024,128]{1,0:T(8,128)S(1)} %bitcast.141), channel_id=1, source_target_pairs={{0,256},{8,264},{16,272},{24,280},{32,288},{40,296},{48,304},{56,3... | collective-permute-start | bytes 1572872 | tf_op jit(solution)/shard_map/ppermute | solution.py:10
  118.9 4.6 scatter_fusion.2
  123.5 1.9 collective-permute-start.5
  125.5 2.6 scatter_fusion.3
  128.1 1.9 collective-permute-start.6
  130.1 4.6 scatter_fusion.4
  134.7 1.9 collective-permute-start.7
  136.6 3.2 fusion.14
  139.9 4.6 scatter_fusion
  144.5 8.2 %collective-permute-done.4 = f32[1024,128]{1,0:T(8,128)} collective-permute-done((f32[1024,128]{1,0:T(8,128)S(1)}, f32[1024,128]{1,0:T(8,128)}, u32[]{:S(2)}, u32[]{:S(2)}) %collective-permute-start.4) | collective-permute-done | bytes 524320 | tf_op jit(solution)/shard_map/ppermute | solution.py:10
  152.6 51.6 %collective-permute-done.5 = f32[1024,128]{1,0:T(8,128)} collective-permute-done((f32[1024,128]{1,0:T(8,128)S(1)}, f32[1024,128]{1,0:T(8,128)}, u32[]{:S(2)}, u32[]{:S(2)}) %collective-permute-start.5) | collective-permute-done | bytes 524320 | tf_op jit(solution)/shard_map/ppermute | solution.py:10
  204.2 2.3 fusion.53
  206.5 114.1 %psum.15 = f32[128]{0:T(128)} all-reduce(f32[128]{0:T(128)S(1)} %get-tuple-element.8), channel_id=1, replica_groups=mesh['dom'=64,'rep'=8] {'dom','rep'}, use_global_device_ids=true, to_apply=%region_8.9 | all-reduce | flops 128 | bytes 1024 | tf_op jit(solution)/shard_map/psum | solution.py:78
  320.7 1.7 convolution_bitcast_fusion.5
  324.0 438.2 %all-reduce.2.cloned.1.call-done = f32[128,128]{0,1:T(8,128)} async-done(((f32[128,128]{0,1:T(8,128)}), f32[128,128]{0,1:T(8,128)}) %all-reduce.2.cloned.1.call-update) | async-done | bytes 65552 | tf_op jit(solution)/shard_map/psum | solution.py:78
  (39 shorter events, 10.9 us)
Async XLA Ops:
  7.2 0.8 copy-start
  7.2 313.5 %reduce-scatter.2.cloned.1.call-start = ((), (), s32[]{:S(2)}) async-start(), calls=%async_computation.1 | async-start | bytes 589824 | tf_op jit(solution)/shard_map/reduce_scatter | solution.py:71
  28.3 24.9 %collective-permute-start.3 = (bf16[1024,128]{1,0:T(8,128)(2,1)S(1)}, bf16[1024,128]{1,0:T(8,128)(2,1)S(1)}, u32[]{:S(2)}, u32[]{:S(2)}) collective-permute-start(bf16[1024,128]{1,0:T(8,128)(2,1)S(1)} %all_gather.3), channel_id=1, source_target_pairs={{0,32},{8,40},{16,48},{24,56},{32,0},{40,8},{48,16},{56,24},{64,96... | collective-permute-start | bytes 786440 | tf_op jit(solution)/shard_map/ppermute | solution.py:10
  30.2 33.4 %collective-permute-start.2 = (bf16[1024,128]{1,0:T(8,128)(2,1)S(1)}, bf16[1024,128]{1,0:T(8,128)(2,1)S(1)}, u32[]{:S(2)}, u32[]{:S(2)}) collective-permute-start(bf16[1024,128]{1,0:T(8,128)(2,1)S(1)} %all_gather.3), channel_id=1, source_target_pairs={{0,64},{8,72},{16,80},{24,88},{32,96},{40,104},{48,112},{56,120},{... | collective-permute-start | bytes 786440 | tf_op jit(solution)/shard_map/ppermute | solution.py:10
  32.2 53.7 %collective-permute-start.1 = (bf16[1024,128]{1,0:T(8,128)(2,1)S(1)}, bf16[1024,128]{1,0:T(8,128)(2,1)S(1)}, u32[]{:S(2)}, u32[]{:S(2)}) collective-permute-start(bf16[1024,128]{1,0:T(8,128)(2,1)S(1)} %all_gather.3), channel_id=1, source_target_pairs={{0,128},{8,136},{16,144},{24,152},{32,160},{40,168},{48,176},{56,1... | collective-permute-start | bytes 786440 | tf_op jit(solution)/shard_map/ppermute | solution.py:10
  40.6 47.7 %collective-permute-start = (bf16[1024,128]{1,0:T(8,128)(2,1)S(1)}, bf16[1024,128]{1,0:T(8,128)(2,1)S(1)}, u32[]{:S(2)}, u32[]{:S(2)}) collective-permute-start(bf16[1024,128]{1,0:T(8,128)(2,1)S(1)} %all_gather.3), channel_id=1, source_target_pairs={{0,256},{8,264},{16,272},{24,280},{32,288},{40,296},{48,304},{56,3... | collective-permute-start | bytes 786440 | tf_op jit(solution)/shard_map/ppermute | solution.py:10
  86.6 2.4 copy-start.2
  86.6 2.4 copy-start.3
  107.6 45.0 %collective-permute-start.4 = (f32[1024,128]{1,0:T(8,128)S(1)}, f32[1024,128]{1,0:T(8,128)}, u32[]{:S(2)}, u32[]{:S(2)}) collective-permute-start(f32[1024,128]{1,0:T(8,128)S(1)} %bitcast.141), channel_id=1, source_target_pairs={{0,256},{8,264},{16,272},{24,280},{32,288},{40,296},{48,304},{56,3... | collective-permute-start | bytes 1572872 | tf_op jit(solution)/shard_map/ppermute | solution.py:10
  123.5 80.7 %collective-permute-start.5 = (f32[1024,128]{1,0:T(8,128)S(1)}, f32[1024,128]{1,0:T(8,128)}, u32[]{:S(2)}, u32[]{:S(2)}) collective-permute-start(f32[1024,128]{1,0:T(8,128)S(1)} %bitcast.142), channel_id=1, source_target_pairs={{0,128},{8,136},{16,144},{24,152},{32,160},{40,168},{48,176},{56,1... | collective-permute-start | bytes 1572872 | tf_op jit(solution)/shard_map/ppermute | solution.py:10
  128.1 76.1 %collective-permute-start.6 = (f32[1024,128]{1,0:T(8,128)S(1)}, f32[1024,128]{1,0:T(8,128)S(1)}, u32[]{:S(2)}, u32[]{:S(2)}) collective-permute-start(f32[1024,128]{1,0:T(8,128)S(1)} %bitcast.143), channel_id=1, source_target_pairs={{0,64},{8,72},{16,80},{24,88},{32,96},{40,104},{48,112},{56,120},{... | collective-permute-start | bytes 1572872 | tf_op jit(solution)/shard_map/ppermute | solution.py:10
  134.7 69.5 %collective-permute-start.7 = (f32[1024,128]{1,0:T(8,128)S(1)}, f32[1024,128]{1,0:T(8,128)}, u32[]{:S(2)}, u32[]{:S(2)}) collective-permute-start(f32[1024,128]{1,0:T(8,128)S(1)} %bitcast.144), channel_id=1, source_target_pairs={{0,32},{8,40},{16,48},{24,56},{32,0},{40,8},{48,16},{56,24},{64,96... | collective-permute-start | bytes 1572872 | tf_op jit(solution)/shard_map/ppermute | solution.py:10
  144.4 177.9 %copy-start.1 = (bf16[128,128]{1,0:T(8,128)(2,1)S(1)}, bf16[128,128]{1,0:T(8,128)(2,1)}, u32[]{:S(2)}) copy-start(bf16[128,128]{1,0:T(8,128)(2,1)} %param.8) | copy-start | bytes 98308
  206.5 555.7 %all-reduce.2.cloned.1.call-start = ((), (), s32[]{:S(2)}) async-start(), calls=%async_computation.2 | async-start | bytes 131072 | tf_op jit(solution)/shard_map/psum | solution.py:78
Sparse Core Ops, SparseCore 0:
  206.6 44.0 reduce-scatter.1
  322.5 439.6 all-reduce.1
where the time goes:
time: 772 us; the launch traced here: 771 us
  waiting for transfers between devices  526 us (68%)
  blocking collectives  134 us (17%)
  starting transfers between devices  37.3 us (5%)
  matrix products  27.8 us (4%)
  other arithmetic  25.4 us (3%)
  between operations  14.3 us (2%)
    psum x1, waiting for transfers between devices, body(): lax.psum((weight_local, bias_local), ('dom', 'rep'))  438 us
    psum x1, blocking collectives, body(): lax.psum((weight_local, bias_local), ('dom', 'rep'))  114 us
    ppermute x8, waiting for transfers between devices, swapped(): return lax.ppermute(value, axis, pairs)  87.7 us
    ppermute x8, starting transfers between devices, swapped(): return lax.ppermute(value, axis, pairs)  37.2 us
    scatter-add x5, other arithmetic, partial_panel(): placed.at[targets]  20.9 us
    all_gather x1, blocking collectives, body(): own_rows = lax.all_gather(projected, 'rep', axis=0, tiled=True)  19.5 us
  transfers between devices with their start and end apart: 10, of which 5 were waited for; matrix products, arithmetic and copies ran while one was open for 4% of the time, Pallas kernels for 0%

commit v1 on v0

--- a/solution.py
+++ b/solution.py
@@ -2,6 +2,12 @@
 import jax.numpy as jnp
 from jax import lax
 from jax.sharding import PartitionSpec as P
+
+
+def draw_outputs(content):
+    for m in ("rep", "dom"):
+        content = lax.psum(content, m)
+    return content
 
 
 def swapped(value, axis, bit):
@@ -75,7 +81,7 @@
         feats, grad_proj, (((0,), (0,)), ((), ())), preferred_element_type=jnp.float32
     )
     bias_local = jnp.sum(grad_pre, axis=0)
-    grad_weight, grad_bias = lax.psum((weight_local, bias_local), ("dom", "rep"))
+    grad_weight, grad_bias = draw_outputs((weight_local, bias_local))
     grad_feats = lax.dot_general(
         grad_proj, weight, (((1,), (1,)), ((), ())), preferred_element_type=jnp.float32
     ).astype(jnp.bfloat16)

time: 772 us -> 676 us (0.88); the launches traced: 771 us -> 664 us
  waiting for transfers between devices: 526 us -> 402 us
  blocking collectives: 134 us -> 151 us
    psum x1 -> x2, waiting for transfers between devices: 438 us -> 270 us  [draw_outputs(): content = lax.psum(content, m)]
    reduce_scatter x1, waiting for transfers between devices: 0.01 us -> 44.2 us  [body(): lax.psum_scatter(grad_panel, 'rep', scatter_dimension=0, tiled=True)]
    psum x1 -> x2, blocking collectives: 114 us -> 131 us  [draw_outputs(): content = lax.psum(content, m)]
  transfers between devices with their start and end apart: 10 -> 11, of which waited for: 5 -> 6; matrix products, arithmetic and copies ran while one was open for 4% -> 5% of each run, Pallas kernels for 0% -> 0%
where the time goes in v1:
time: 676 us; the launch traced here: 664 us
  waiting for transfers between devices  402 us (59%)
  blocking collectives  151 us (22%)
  starting transfers between devices  37.4 us (6%)
  matrix products  27.8 us (4%)
  other arithmetic  25.4 us (4%)
  between operations  14 us (2%)
    psum x2, waiting for transfers between devices, draw_outputs(): content = lax.psum(content, m)  270 us
    psum x2, blocking collectives, draw_outputs(): content = lax.psum(content, m)  131 us
    ppermute x8, waiting for transfers between devices, swapped(): return lax.ppermute(value, axis, pairs)  87.7 us
    reduce_scatter x1, waiting for transfers between devices, body(): lax.psum_scatter(grad_panel, 'rep', scatter_dimension=0, tiled=True)  44.2 us
    ppermute x8, starting transfers between devices, swapped(): return lax.ppermute(value, axis, pairs)  37.2 us
    scatter-add x5, other arithmetic, partial_panel(): placed.at[targets]  20.9 us
    all_gather x1, blocking collectives, body(): own_rows = lax.all_gather(projected, 'rep', axis=0, tiled=True)  19.5 us
    dot_general x5, matrix products, partial_panel(): jnp.einsum('tmij,tih->tmjh', masked, grad_rows_b, preferred_element_type=...  14.8 us
  transfers between devices with their start and end apart: 11, of which 6 were waited for; matrix products, arithmetic and copies ran while one was open for 5% of the time, Pallas kernels for 0%

profile of v1, /device:TPU:1, one launch (start us, length us, event | category | flops | bytes accessed | tf_op | source)
XLA Modules:
  0.0 663.9 jit_solution(14139815691807882995)
XLA Ops:
  8.8 19.5 %all_gather.3 = bf16[1024,128]{1,0:T(8,128)(2,1)S(1)} all-gather(bf16[128,128]{1,0:T(8,128)(2,1)S(1)} %convolution_convert_fusion.1), channel_id=1, replica_groups=mesh['dom'=64,'rep'=8] {'rep'}, dimensions={0}, use_global_device_ids=true | all-gather | bytes 294912 | tf_op jit(solution)/shard_map/all_gather | solution.py:59
  28.3 1.9 collective-permute-start.3
  30.2 1.9 collective-permute-start.2
  32.2 8.4 %collective-permute-start.1 = (bf16[1024,128]{1,0:T(8,128)(2,1)S(1)}, bf16[1024,128]{1,0:T(8,128)(2,1)S(1)}, u32[]{:S(2)}, u32[]{:S(2)}) collective-permute-start(bf16[1024,128]{1,0:T(8,128)(2,1)S(1)} %all_gather.3), channel_id=1, source_target_pairs={{0,128},{8,136},{16,144},{24,152},{32,160},{40,168},{48,176},{56,1... | collective-permute-start | bytes 786440 | tf_op jit(solution)/shard_map/ppermute | solution.py:16
  40.6 7.9 %collective-permute-start = (bf16[1024,128]{1,0:T(8,128)(2,1)S(1)}, bf16[1024,128]{1,0:T(8,128)(2,1)S(1)}, u32[]{:S(2)}, u32[]{:S(2)}) collective-permute-start(bf16[1024,128]{1,0:T(8,128)(2,1)S(1)} %all_gather.3), channel_id=1, source_target_pairs={{0,256},{8,264},{16,272},{24,280},{32,288},{40,296},{48,304},{56,3... | collective-permute-start | bytes 786440 | tf_op jit(solution)/shard_map/ppermute | solution.py:16
  55.6 8.0 %collective-permute-done.2 = bf16[1024,128]{1,0:T(8,128)(2,1)S(1)} collective-permute-done((bf16[1024,128]{1,0:T(8,128)(2,1)S(1)}, bf16[1024,128]{1,0:T(8,128)(2,1)S(1)}, u32[]{:S(2)}, u32[]{:S(2)}) %collective-permute-start.2) | collective-permute-done | bytes 262176 | tf_op jit(solution)/shard_map/ppermute | solution.py:16
  64.3 1.6 convolution_bitcast_fusion.1
  66.0 19.9 %collective-permute-done.1 = bf16[1024,128]{1,0:T(8,128)(2,1)S(1)} collective-permute-done((bf16[1024,128]{1,0:T(8,128)(2,1)S(1)}, bf16[1024,128]{1,0:T(8,128)(2,1)S(1)}, u32[]{:S(2)}, u32[]{:S(2)}) %collective-permute-start.1) | collective-permute-done | bytes 262176 | tf_op jit(solution)/shard_map/ppermute | solution.py:16
  86.7 1.6 convolution_bitcast_fusion.2
  89.1 2.3 fusion.100
  91.4 3.2 fusion.12
  94.6 3.2 fusion.10
  97.8 2.0 fusion.8
  99.8 3.2 fusion.6
  103.0 4.6 scatter_fusion.1
  107.6 11.3 %collective-permute-start.4 = (f32[1024,128]{1,0:T(8,128)S(1)}, f32[1024,128]{1,0:T(8,128)}, u32[]{:S(2)}, u32[]{:S(2)}) collective-permute-start(f32[1024,128]{1,0:T(8,128)S(1)} %bitcast.141), channel_id=1, source_target_pairs={{0,256},{8,264},{16,272},{24,280},{32,288},{40,296},{48,304},{56,3... | collective-permute-start | bytes 1572872 | tf_op jit(solution)/shard_map/ppermute | solution.py:16
  118.9 4.6 scatter_fusion.2
  123.5 1.9 collective-permute-start.5
  125.5 2.6 scatter_fusion.3
  128.1 1.9 collective-permute-start.6
  130.1 4.6 scatter_fusion.4
  134.7 1.9 collective-permute-start.7
  136.6 3.2 fusion.14
  139.9 4.6 scatter_fusion
  144.5 8.2 %collective-permute-done.4 = f32[1024,128]{1,0:T(8,128)} collective-permute-done((f32[1024,128]{1,0:T(8,128)S(1)}, f32[1024,128]{1,0:T(8,128)}, u32[]{:S(2)}, u32[]{:S(2)}) %collective-permute-start.4) | collective-permute-done | bytes 524320 | tf_op jit(solution)/shard_map/ppermute | solution.py:16
  152.6 51.6 %collective-permute-done.5 = f32[1024,128]{1,0:T(8,128)} collective-permute-done((f32[1024,128]{1,0:T(8,128)S(1)}, f32[1024,128]{1,0:T(8,128)}, u32[]{:S(2)}, u32[]{:S(2)}) %collective-permute-start.5) | collective-permute-done | bytes 524320 | tf_op jit(solution)/shard_map/ppermute | solution.py:16
  204.2 2.3 fusion.53
  206.5 44.2 %reduce-scatter.2.cloned.1.call-done = f32[128,128]{1,0:T(8,128)} async-done(((f32[1024,128]{1,0:T(8,128)}), f32[128,128]{1,0:T(8,128)}) %reduce-scatter.2.cloned.1.call-update) | async-done | bytes 65552 | tf_op jit(solution)/shard_map/reduce_scatter | solution.py:77
  250.7 1.7 convolution_bitcast_fusion.5
  252.4 13.9 %psum.30 = f32[128]{0:T(128)S(1)} all-reduce(f32[128]{0:T(128)S(1)} %get-tuple-element.8), channel_id=1, replica_groups=mesh['dom'=64,'rep'=8] {'rep'}, use_global_device_ids=true, to_apply=%region_9.10 | all-reduce | flops 128 | bytes 1024 | tf_op jit(solution)/shard_map/psum | solution.py:9
  266.3 117.4 %psum.31 = f32[128]{0:T(128)} all-reduce(f32[128]{0:T(128)S(1)} %psum.30), channel_id=1, replica_groups=mesh['dom'=64,'rep'=8] {'dom'}, use_global_device_ids=true, to_apply=%region_10.11 | all-reduce | flops 128 | bytes 1024 | tf_op jit(solution)/shard_map/psum | solution.py:9
  385.4 270.4 %all-reduce.5.cloned.1.call-done = f32[128,128]{0,1:T(8,128)} async-done(((f32[128,128]{0,1:T(8,128)}), f32[128,128]{0,1:T(8,128)}) %all-reduce.5.cloned.1.call-update) | async-done | bytes 65552 | tf_op jit(solution)/shard_map/psum | solution.py:9
  (43 shorter events, 14.3 us)
Async XLA Ops:
  7.2 0.8 copy-start
  7.2 243.5 %reduce-scatter.2.cloned.1.call-start = ((), (), s32[]{:S(2)}) async-start(), calls=%async_computation.1 | async-start | bytes 589824 | tf_op jit(solution)/shard_map/reduce_scatter | solution.py:77
  28.3 24.9 %collective-permute-start.3 = (bf16[1024,128]{1,0:T(8,128)(2,1)S(1)}, bf16[1024,128]{1,0:T(8,128)(2,1)S(1)}, u32[]{:S(2)}, u32[]{:S(2)}) collective-permute-start(bf16[1024,128]{1,0:T(8,128)(2,1)S(1)} %all_gather.3), channel_id=1, source_target_pairs={{0,32},{8,40},{16,48},{24,56},{32,0},{40,8},{48,16},{56,24},{64,96... | collective-permute-start | bytes 786440 | tf_op jit(solution)/shard_map/ppermute | solution.py:16
  30.2 33.4 %collective-permute-start.2 = (bf16[1024,128]{1,0:T(8,128)(2,1)S(1)}, bf16[1024,128]{1,0:T(8,128)(2,1)S(1)}, u32[]{:S(2)}, u32[]{:S(2)}) collective-permute-start(bf16[1024,128]{1,0:T(8,128)(2,1)S(1)} %all_gather.3), channel_id=1, source_target_pairs={{0,64},{8,72},{16,80},{24,88},{32,96},{40,104},{48,112},{56,120},{... | collective-permute-start | bytes 786440 | tf_op jit(solution)/shard_map/ppermute | solution.py:16
  32.2 53.7 %collective-permute-start.1 = (bf16[1024,128]{1,0:T(8,128)(2,1)S(1)}, bf16[1024,128]{1,0:T(8,128)(2,1)S(1)}, u32[]{:S(2)}, u32[]{:S(2)}) collective-permute-start(bf16[1024,128]{1,0:T(8,128)(2,1)S(1)} %all_gather.3), channel_id=1, source_target_pairs={{0,128},{8,136},{16,144},{24,152},{32,160},{40,168},{48,176},{56,1... | collective-permute-start | bytes 786440 | tf_op jit(solution)/shard_map/ppermute | solution.py:16
  40.6 47.7 %collective-permute-start = (bf16[1024,128]{1,0:T(8,128)(2,1)S(1)}, bf16[1024,128]{1,0:T(8,128)(2,1)S(1)}, u32[]{:S(2)}, u32[]{:S(2)}) collective-permute-start(bf16[1024,128]{1,0:T(8,128)(2,1)S(1)} %all_gather.3), channel_id=1, source_target_pairs={{0,256},{8,264},{16,272},{24,280},{32,288},{40,296},{48,304},{56,3... | collective-permute-start | bytes 786440 | tf_op jit(solution)/shard_map/ppermute | solution.py:16
  86.6 2.4 copy-start.2
  86.6 2.4 copy-start.3
  107.6 45.0 %collective-permute-start.4 = (f32[1024,128]{1,0:T(8,128)S(1)}, f32[1024,128]{1,0:T(8,128)}, u32[]{:S(2)}, u32[]{:S(2)}) collective-permute-start(f32[1024,128]{1,0:T(8,128)S(1)} %bitcast.141), channel_id=1, source_target_pairs={{0,256},{8,264},{16,272},{24,280},{32,288},{40,296},{48,304},{56,3... | collective-permute-start | bytes 1572872 | tf_op jit(solution)/shard_map/ppermute | solution.py:16
  123.5 80.7 %collective-permute-start.5 = (f32[1024,128]{1,0:T(8,128)S(1)}, f32[1024,128]{1,0:T(8,128)}, u32[]{:S(2)}, u32[]{:S(2)}) collective-permute-start(f32[1024,128]{1,0:T(8,128)S(1)} %bitcast.142), channel_id=1, source_target_pairs={{0,128},{8,136},{16,144},{24,152},{32,160},{40,168},{48,176},{56,1... | collective-permute-start | bytes 1572872 | tf_op jit(solution)/shard_map/ppermute | solution.py:16
  128.1 76.1 %collective-permute-start.6 = (f32[1024,128]{1,0:T(8,128)S(1)}, f32[1024,128]{1,0:T(8,128)S(1)}, u32[]{:S(2)}, u32[]{:S(2)}) collective-permute-start(f32[1024,128]{1,0:T(8,128)S(1)} %bitcast.143), channel_id=1, source_target_pairs={{0,64},{8,72},{16,80},{24,88},{32,96},{40,104},{48,112},{56,120},{... | collective-permute-start | bytes 1572872 | tf_op jit(solution)/shard_map/ppermute | solution.py:16
  134.7 69.5 %collective-permute-start.7 = (f32[1024,128]{1,0:T(8,128)S(1)}, f32[1024,128]{1,0:T(8,128)}, u32[]{:S(2)}, u32[]{:S(2)}) collective-permute-start(f32[1024,128]{1,0:T(8,128)S(1)} %bitcast.144), channel_id=1, source_target_pairs={{0,32},{8,40},{16,48},{24,56},{32,0},{40,8},{48,16},{56,24},{64,96... | collective-permute-start | bytes 1572872 | tf_op jit(solution)/shard_map/ppermute | solution.py:16
  144.4 239.3 %copy-start.1 = (bf16[128,128]{1,0:T(8,128)(2,1)S(1)}, bf16[128,128]{1,0:T(8,128)(2,1)}, u32[]{:S(2)}) copy-start(bf16[128,128]{1,0:T(8,128)(2,1)} %param.8) | copy-start | bytes 98308
  206.5 177.2 %all-reduce.3.cloned.1.call-start = ((), (), s32[]{:S(2)}) async-start(), calls=%async_computation.2 | async-start | bytes 131072 | tf_op jit(solution)/shard_map/psum | solution.py:9
  252.4 403.4 %all-reduce.5.cloned.1.call-start = ((), (), s32[]{:S(2)}) async-start(), calls=%async_computation.3 | async-start | bytes 131072 | tf_op jit(solution)/shard_map/psum | solution.py:9
Sparse Core Ops, SparseCore 0:
  206.6 44.0 reduce-scatter.1
  253.6 74.1 all-reduce.2
  383.9 271.9 all-reduce.4
